TPU v7x, 512 devices: a whole 4x4x16 slice. The times are simulated.
512 devices in a mesh: region: 16 (over y, x), tile: 32 (over z, core).
Axes of the slice: x: 4, y: 4, z: 16, core: 2. Of those that a mesh axis runs over, the one named last changes fastest.
Arguments:
- density: float32 [16, 1024, 1024], P('region', 'tile'), may hold values from -48 to 56, as said below
- atom_xyz: float32 [16, 3, 256], P('region'), may hold values from 0 to 3
- atom_of: int32 [16, 1024], P('region'), may hold values from 0 to 255
- exponent: float32 [16, 1024], P('region'), may hold values from 0.1 to 1
- points: float32 [1024, 3, 512], P(('region', 'tile')), may hold values from 0 to 3
- weights: float32 [1024, 512], P(('region', 'tile')), may hold values from 6.1035156e-05 to 0.00018310547
- lists: int32 [1024, 4], P(('region', 'tile')), may hold values from 0 to 7, all different within a row
- live: int32 [512], P(('region', 'tile')), may hold values from 1 to 2, as said below
Outputs:
- potential: float32 [16, 1024, 1024], P('region', 'tile')
Inputs may be any that keep to these rules, and one draw needn't show every extreme that they name: `density`: each region's matrix is symmetric and positive definite. `lists`: each row names 4 different blocks of its own region. a device's slots 0 to live - 1 hold its live batches and the others are unused; some device has 2.
All inputs are finite; a program needn't handle non-finite values.
Results may differ from a plain program's by a relative error of at most 0.0003.
Values sent between devices are 32-bit elements; how exact they have to be, the bound alone decides.
No kernel may reach another device: no remote copies, remote signals or barrier semaphores. Data moves between devices by JAX's collectives and lax.ppermute only.
A program may use at most 128 MiB of HBM per device.

v0:
```python
import math
import jax
import jax.numpy as jnp
from jax import lax
from jax.sharding import Mesh
from jax.sharding import PartitionSpec as P

BLK = 128
TILE = ("tile_0", "tile_1")
REGION_TILE = ("region", "tile_0", "tile_1")
slater_coef = (3.0 / math.pi) ** (1.0 / 3.0)
highest = lax.Precision.HIGHEST


def reduced_to_own(tiles, axes, turns):
    lengths = [lax.axis_size(a) for a in axes]
    tiles = tiles.reshape(*lengths, *tiles.shape[1:])
    tiles = tiles.transpose(*turns, *range(len(axes), tiles.ndim))
    tiles = tiles.reshape(-1, *tiles.shape[len(axes) :])
    for k in turns:
        tiles = lax.psum_scatter(tiles, axes[k], scatter_dimension=0, tiled=True)
    return tiles[0]


def cut_along(value, dim, size):
    lengths = value.shape
    tiles = value.reshape(*lengths[:dim], size, lengths[dim] // size, *lengths[dim + 1 :])
    return jnp.moveaxis(tiles, dim, 0)


def scatter_axes(value, axes, turns, dim):
    size = lax.axis_size(axes)
    return reduced_to_own(cut_along(value, dim, size), axes, turns)


def expand_blocks(blocks):
    inner = jnp.arange(BLK, dtype=jnp.int32)
    full = blocks[..., :, None] * BLK + inner
    return full.reshape(blocks.shape[:-1] + (blocks.shape[-1] * BLK,))


def gather_block(region_density, blocks):
    block_total = region_density.shape[0] // BLK
    count = blocks.shape[0]
    tiled = region_density.reshape(block_total, BLK, block_total, BLK)
    picked = jnp.take(jnp.take(tiled, blocks, axis=0), blocks, axis=2)
    return picked.reshape(count * BLK, count * BLK)


def add_term(running, blocks, batch_result):
    block_total = running.shape[1] // BLK
    count = blocks.shape[0]
    pieces = batch_result.reshape(count, BLK, count, BLK)
    for row_block in range(count):
        start = blocks[row_block] * BLK
        slab = lax.dynamic_slice_in_dim(running, start, BLK, 0).reshape(BLK, block_total, BLK)
        slab = slab.at[:, blocks, :].add(pieces[row_block])
        running = lax.dynamic_update_slice_in_dim(
            running, slab.reshape(BLK, block_total * BLK), start, 0
        )
    return running


def orbital_matrix(coords, centers, exponents):
    distance = jnp.zeros((coords.shape[1], centers.shape[1]), jnp.float32)
    for axis_no in range(3):
        offset = coords[axis_no][:, None] - centers[axis_no][None, :]
        distance = distance + offset * offset
    return jnp.exp(-exponents[None, :] * distance)


def batch_term(coords, weight, centers, exponents, block_density):
    orbital = orbital_matrix(coords, centers, exponents)
    mixed = jnp.dot(orbital, block_density, precision=highest, preferred_element_type=jnp.float32)
    point_density = jnp.sum(orbital * mixed, axis=1)
    factor = weight * -slater_coef * jnp.cbrt(point_density)
    return lax.dot_general(
        orbital,
        orbital * factor[:, None],
        (((0,), (0,)), ((), ())),
        precision=highest,
        preferred_element_type=jnp.float32,
    )


def body(density, atom_xyz, atom_of, exponent, points, weights, lists, live):
    table_xyz = atom_xyz[0]
    atom_index = atom_of[0]
    exponent_row = exponent[0]
    region_density = lax.all_gather(density, TILE, axis=1, tiled=True)[0]
    members_all = expand_blocks(lists)
    centers = jnp.moveaxis(jnp.take(table_xyz, jnp.take(atom_index, members_all), axis=1), 1, 0)
    exponents = jnp.take(exponent_row, members_all)
    own_count = live[0]
    running = jnp.zeros(region_density.shape, jnp.float32)

    def own_batch(slot_no, running):
        blocks = lists[slot_no]
        batch_result = batch_term(
            points[slot_no],
            weights[slot_no],
            centers[slot_no],
            exponents[slot_no],
            gather_block(region_density, blocks),
        )
        return add_term(running, blocks, batch_result)

    running = lax.fori_loop(0, own_count, own_batch, running)
    owned_rows = scatter_axes(running[None], TILE, (1, 0), 1)
    return owned_rows


def solution(mesh):
    torus = Mesh(mesh.devices.reshape(mesh.shape["region"], 16, 2), ("region", "tile_0", "tile_1"))
    return jax.shard_map(
        body,
        mesh=torus,
        in_specs=(
            P("region", TILE, None),
            P("region", None, None),
            P("region", None),
            P("region", None),
            P(REGION_TILE, None, None),
            P(REGION_TILE, None),
            P(REGION_TILE, None),
            P(REGION_TILE),
        ),
        out_specs=P("region", TILE, None),
        check_vma=False,
    )
```

profile of v0, /device:TPU:8, one launch (start us, length us, event | category | flops | bytes accessed | tf_op | source)
XLA Modules:
  0.0 269.8 jit_solution(4212617765108527290)
XLA Ops:
  8.1 4.5 %gather_fusion.3 = s32[1024]{0:T(1024)S(1)} fusion(s32[1024]{0:T(1024)S(1)} %bitcast.149, s32[1024]{0:T(1024)S(1)} %broadcast_clamp_fusion.1), kind=kCustom, calls=%fused_computation.3 | custom fusion | bytes 12288 | tf_op jit(solution)/shard_map/jit(_take)/gather | solution.py:92
  12.9 2.8 %gather_fusion.4 = f32[1024,3]{1,0:T(8,128)S(1)} fusion(f32[3,256]{0,1:T(8,128)S(1)} %bitcast.174, s32[1024]{0:T(1024)S(1)} %broadcast_clamp_fusion), kind=kCustom, calls=%fused_computation.4 | custom fusion | bytes 28672 | tf_op jit(solution)/shard_map/jit(_take)/gather | solution.py:92
  15.9 4.5 %gather_fusion.2 = f32[1024]{0:T(1024)S(1)} fusion(f32[1024]{0:T(1024)S(1)} %bitcast.150, s32[1024]{0:T(1024)S(1)} %broadcast_clamp_fusion.1), kind=kCustom, calls=%fused_computation.2 | custom fusion | bytes 12288 | tf_op jit(solution)/shard_map/jit(_take)/gather | solution.py:93
  20.6 66.7 %all-gather.2.cloned.1.call-done = f32[1,1024,1024]{2,1,0:T(8,128)} async-done(((f32[1,32,1024]{2,1,0:T(8,128)}), f32[1,1024,1024]{2,1,0:T(8,128)}) %all-gather.2.cloned.1.call-update) | async-done | bytes 4194320 | tf_op jit(solution)/shard_map/all_gather | solution.py:90
  87.2 2.5 broadcast_in_dim.58
  89.8 65.6 %while.10 = (s32[]{:T(128)}, f32[1024,1024]{0,1:T(8,128)}, s32[]{:T(128)}, s32[2,4]{1,0:T(2,128)S(1)}, f32[2,512]{1,0:T(2,128)S(1)}, /*index=5*/f32[2,3,512]{2,0...) while((s32[]{:T(128)}, f32[1024,1024]{0,1:T(8,128)}, ...), condition=%wide.region_6.7_spmd, body=%wide.region_0.6_spmd.sunk | while | flops 3230140416 | bytes 51457692 | solution.py:108
  90.5 5.1 %copy.95 = f32[128,8,8,128]{3,2,1,0:T(8,128)} copy(f32[128,8,8,128]{3,1,2,0:T(8,128)} %bitcast.152) | data formatting | bytes 8388608 | tf_op jit(solution)/shard_map/while
  95.6 2.9 %gather_fusion = f32[4,128,8,128]{3,2,1,0:T(8,128)S(1)} fusion(f32[8,128,8,128]{3,2,1,0:T(8,128)} %bitcast.151, s32[1024]{0:T(1024)S(1)} %pad_clamp_fusion.2), kind=kCustom, calls=%fused_computation.clone.1 | custom fusion | bytes 4194320 | tf_op jit(solution)/shard_map/while/body/jit(_take)/gather | solution.py:46
  100.5 2.6 fusion.40
  103.2 2.7 fusion.41
  107.4 1.1 constant_dynamic-slice_fusion.20
  109.6 0.9 constant_dynamic-update-slice_fusion.8
  111.2 1.1 constant_dynamic-slice_fusion.23
  113.6 0.9 constant_dynamic-update-slice_fusion.9
  115.0 1.1 constant_dynamic-slice_fusion.24
  117.4 0.9 constant_dynamic-update-slice_fusion.10
  118.9 1.1 constant_dynamic-slice_fusion.25
  121.3 0.9 constant_dynamic-update-slice_fusion.11
  122.9 5.1 %copy.95 = f32[128,8,8,128]{3,2,1,0:T(8,128)} copy(f32[128,8,8,128]{3,1,2,0:T(8,128)} %bitcast.152) | data formatting | bytes 8388608 | tf_op jit(solution)/shard_map/while
  128.1 2.9 %gather_fusion = f32[4,128,8,128]{3,2,1,0:T(8,128)S(1)} fusion(f32[8,128,8,128]{3,2,1,0:T(8,128)} %bitcast.151, s32[1024]{0:T(1024)S(1)} %pad_clamp_fusion.2), kind=kCustom, calls=%fused_computation.clone.1 | custom fusion | bytes 4194320 | tf_op jit(solution)/shard_map/while/body/jit(_take)/gather | solution.py:46
  133.0 2.6 fusion.40
  135.7 2.7 fusion.41
  139.8 1.1 constant_dynamic-slice_fusion.20
  142.1 0.9 constant_dynamic-update-slice_fusion.8
  143.7 1.1 constant_dynamic-slice_fusion.23
  147.5 1.1 constant_dynamic-slice_fusion.24
  151.4 1.1 constant_dynamic-slice_fusion.25
  153.8 0.9 constant_dynamic-update-slice_fusion.11
  155.3 5.4 %copy.64 = f32[1024,1024]{1,0:T(8,128)} copy(f32[1024,1024]{0,1:T(8,128)} %get-tuple-element.53) | data formatting | bytes 8388608 | tf_op jit(solution)/shard_map/while | solution.py:108
  160.7 4.7 %copy.65 = f32[2,16,1,32,1024]{4,3,1,0,2:T(8,128)} copy(f32[2,16,1,32,1024]{4,3,0,1,2:T(8,128)} %bitcast.172) | data formatting | bytes 8388608 | tf_op jit(solution)/shard_map/transpose | solution.py:18
  165.5 19.4 %reduce-scatter.3.cloned.1.call-done = f32[16,1,32,1024]{3,2,0,1:T(8,128)} async-done(((f32[32,1,32,1024]{3,2,0,1:T(8,128)}), f32[16,1,32,1024]{3,2,0,1:T(8,128)}) %reduce-scatter.3.cloned.1.call-update) | async-done | bytes 2097168 | tf_op jit(solution)/shard_map/reduce_scatter | solution.py:21
  184.9 78.4 %reduce-scatter.5.cloned.1.call-done = f32[1,1,32,1024]{3,2,0,1:T(8,128)} async-done(((f32[16,1,32,1024]{3,2,0,1:T(8,128)}), f32[1,1,32,1024]{3,2,0,1:T(8,128)}) %reduce-scatter.5.cloned.1.call-update) | async-done | bytes 131088 | tf_op jit(solution)/shard_map/reduce_scatter | solution.py:21
  (99 shorter events, 19.6 us)
Async XLA Ops:
  6.5 1.6 copy-start
  6.5 6.2 %copy-start.5 = (f32[1,3,256]{2,0,1:T(1,128)S(1)}, f32[1,3,256]{2,0,1:T(1,128)}, u32[]{:S(2)}) copy-start(f32[1,3,256]{2,0,1:T(1,128)} %param.11) | copy-start | bytes 9220
  6.5 9.4 %copy-start.1 = (f32[1,1024]{1,0:T(1,128)S(1)}, f32[1,1024]{1,0:T(1,128)}, u32[]{:S(2)}) copy-start(f32[1,1024]{1,0:T(1,128)} %param.13) | copy-start | bytes 12292
  6.5 80.7 %all-gather.2.cloned.1.call-start = ((), (), s32[]{:S(2)}) async-start(), calls=%async_computation.2 | async-start | bytes 4325376 | tf_op jit(solution)/shard_map/all_gather | solution.py:90
  7.3 177.6 %reduce-scatter.3.cloned.1.call-start = ((), (), s32[]{:S(2)}) async-start(), calls=%async_computation.3 | async-start | bytes 6291456 | tf_op jit(solution)/shard_map/reduce_scatter | solution.py:21
  15.9 73.9 %copy-start.2 = (f32[2,3,512]{2,0,1:T(2,128)S(1)}, f32[2,3,512]{2,0,1:T(2,128)}, u32[]{:S(2)}) copy-start(f32[2,3,512]{2,0,1:T(2,128)} %param.14) | copy-start | bytes 36868
  15.9 73.9 %copy-start.3 = (f32[2,512]{1,0:T(2,128)S(1)}, f32[2,512]{1,0:T(2,128)}, u32[]{:S(2)}) copy-start(f32[2,512]{1,0:T(2,128)} %param.15) | copy-start | bytes 12292
  15.9 73.8 %copy-start.4 = (s32[2,4]{1,0:T(2,128)S(1)}, s32[2,4]{1,0:T(2,128)}, u32[]{:S(2)}) copy-start(s32[2,4]{1,0:T(2,128)} %param.16) | copy-start | bytes 100
  165.4 97.8 %reduce-scatter.5.cloned.1.call-start = ((), (), s32[]{:S(2)}) async-start(), calls=%async_computation.4 | async-start | bytes 2228224 | tf_op jit(solution)/shard_map/reduce_scatter | solution.py:21
Sparse Core Ops, SparseCore 0:
  9.5 77.7 all-gather.1
  165.6 19.2 reduce-scatter.2
  187.7 75.5 reduce-scatter.4
where the time goes:
time: 271 us; the launch traced here: 270 us
  waiting for transfers between devices  165 us (61%)
  local copies, waits for them, and re-layouts  65.9 us (24%)
  between operations  13.3 us (5%)
  matrix products  10.6 us (4%)
  loops' own time  7.47 us (3%)
  other arithmetic  7.3 us (3%)
    reduce_scatter x2, waiting for transfers between devices, reduced_to_own(): tiles = lax.psum_scatter(tiles, axes[k], scatter_dimension=0, tiled=True)  97.7 us
    all_gather x1, waiting for transfers between devices, body(): region_density = lax.all_gather(density, TILE, axis=1, tiled=True)[0]  66.7 us
    while x2, local copies, waits for them, and re-layouts  10.3 us
    dynamic_slice x8, local copies, waits for them, and re-layouts, add_term(): lax.dynamic_slice_in_dim(running, start, BLK, 0)  8.65 us
    gather x6, local copies, waits for them, and re-layouts, gather_block(): picked = jnp.take(jnp.take(tiled, blocks, axis=0), blocks, axis=2)  8.32 us
    another operation x1, loops' own time, body(): running = lax.fori_loop(0, own_count, own_batch, running)  7.47 us
    dynamic_update_slice x8, local copies, waits for them, and re-layouts, add_term(): lax.dynamic_update_slice_in_dim(running, slab.reshape(BLK, block_total *...  7.07 us
    scatter-add x8, other arithmetic, add_term(): slab = slab.at[:, blocks, :].add(pieces[row_block])  6.02 us
  transfers between devices with their start and end apart: 3, of which 3 were waited for; matrix products, arithmetic and copies ran while one was open for 5% of the time, Pallas kernels for 0%

commit v1 on v0

--- a/solution.py
+++ b/solution.py
@@ -87,7 +87,15 @@
     table_xyz = atom_xyz[0]
     atom_index = atom_of[0]
     exponent_row = exponent[0]
-    region_density = lax.all_gather(density, TILE, axis=1, tiled=True)[0]
+    region_density = jnp.concatenate(
+        jax.lax.all_to_all(
+            jnp.stack([density for _ in range(jax.lax.axis_size(TILE))]),
+            TILE,
+            split_axis=0,
+            concat_axis=0,
+        ),
+        axis=1,
+    )[0]
     members_all = expand_blocks(lists)
     centers = jnp.moveaxis(jnp.take(table_xyz, jnp.take(atom_index, members_all), axis=1), 1, 0)
     exponents = jnp.take(exponent_row, members_all)

time: 271 us -> 395 us (1.46)
  the two profiles are of different devices: /device:TPU:8 before, /device:TPU:10 now
where the time goes in v1:
time: 395 us; the launch traced here: 394 us
  waiting for transfers between devices  271 us (69%)
  local copies, waits for them, and re-layouts  69.2 us (18%)
  starting transfers between devices  15.8 us (4%)
  between operations  13.6 us (3%)
  matrix products  10.6 us (3%)
  loops' own time  7.38 us (2%)
  other arithmetic  6.62 us (2%)
    all_to_all x1, waiting for transfers between devices, body(): jax.lax.all_to_all(jnp.stack([density for _ in range(jax.lax.axis_size(TI...  171 us
    reduce_scatter x2, waiting for transfers between devices, reduced_to_own(): tiles = lax.psum_scatter(tiles, axes[k], scatter_dimension=0, tiled=True)  100 us
    all_to_all x1, starting transfers between devices, body(): jax.lax.all_to_all(jnp.stack([density for _ in range(jax.lax.axis_size(TI...  15.7 us
    while x2, local copies, waits for them, and re-layouts  10.3 us
    dynamic_slice x8, local copies, waits for them, and re-layouts, add_term(): lax.dynamic_slice_in_dim(running, start, BLK, 0)  8.66 us
    gather x6, local copies, waits for them, and re-layouts, gather_block(): picked = jnp.take(jnp.take(tiled, blocks, axis=0), blocks, axis=2)  8.32 us
  transfers between devices with their start and end apart: 3, of which 3 were waited for; matrix products, arithmetic and copies ran while one was open for 3% of the time, Pallas kernels for 0%

profile of v1, /device:TPU:10, one launch (start us, length us, event | category | flops | bytes accessed | tf_op | source)
XLA Modules:
  0.0 394.1 jit_solution(7343746485088691261)
XLA Ops:
  6.5 3.4 stack.2
  9.9 15.7 %all-to-all-start = ((f32[32,1,32,1024]{3,2,1,0:T(8,128)}), f32[32,1,32,1024]{3,2,1,0:T(8,128)}, u32[]{:S(2)}, u32[]{:S(2)}) async-start(f32[32,1,32,1024]{3,2,1,0:T(8,128)} %stack.2), calls=%async_computation | async-start | bytes 8388608 | tf_op jit(solution)/shard_map/all_to_all | solution.py:91
  25.9 4.5 %gather_fusion.3 = s32[1024]{0:T(1024)S(1)} fusion(s32[1024]{0:T(1024)S(1)} %bitcast.153, s32[1024]{0:T(1024)S(1)} %broadcast_clamp_fusion.1), kind=kCustom, calls=%fused_computation.3 | custom fusion | bytes 12288 | tf_op jit(solution)/shard_map/jit(_take)/gather | solution.py:100
  30.7 2.8 gather_fusion.4
  33.7 4.5 %gather_fusion.2 = f32[1024]{0:T(1024)S(1)} fusion(f32[1024]{0:T(1024)S(1)} %bitcast.154, s32[1024]{0:T(1024)S(1)} %broadcast_clamp_fusion.1), kind=kCustom, calls=%fused_computation.2 | custom fusion | bytes 12288 | tf_op jit(solution)/shard_map/jit(_take)/gather | solution.py:101
  38.4 170.8 %all-to-all-done = f32[32,1,32,1024]{3,2,1,0:T(8,128)} async-done(((f32[32,1,32,1024]{3,2,1,0:T(8,128)}), f32[32,1,32,1024]{3,2,1,0:T(8,128)}, u32[]{:S(2)}, u32[]{:S(2)}) %all-to-all-start) | async-done | bytes 4194336 | tf_op jit(solution)/shard_map/all_to_all | solution.py:91
  209.2 2.5 broadcast_in_dim.58
  211.7 65.4 %while.10 = (s32[]{:T(128)}, f32[1024,1024]{0,1:T(8,128)}, s32[]{:T(128)}, s32[2,4]{1,0:T(2,128)S(1)}, f32[2,512]{1,0:T(2,128)S(1)}, /*index=5*/f32[2,3,512]{2,0...) while((s32[]{:T(128)}, f32[1024,1024]{0,1:T(8,128)}, ...), condition=%wide.region_6.7_spmd, body=%wide.region_0.6_spmd.sunk | while | flops 3230140416 | bytes 51457692 | solution.py:116
  212.4 5.2 %copy.114 = f32[128,8,8,128]{3,2,1,0:T(8,128)} copy(f32[128,8,8,128]{3,1,2,0:T(8,128)} %bitcast.124) | data formatting | bytes 8388608 | tf_op jit(solution)/shard_map/while
  217.5 2.9 gather_fusion
  222.5 2.6 fusion.40
  225.1 2.7 fusion.41
  229.3 1.1 constant_dynamic-slice_fusion.20
  231.6 0.9 constant_dynamic-update-slice_fusion.8
  233.0 1.1 constant_dynamic-slice_fusion.23
  236.9 1.1 constant_dynamic-slice_fusion.24
  240.8 1.1 constant_dynamic-slice_fusion.25
  243.1 0.9 constant_dynamic-update-slice_fusion.11
  244.8 5.2 %copy.114 = f32[128,8,8,128]{3,2,1,0:T(8,128)} copy(f32[128,8,8,128]{3,1,2,0:T(8,128)} %bitcast.124) | data formatting | bytes 8388608 | tf_op jit(solution)/shard_map/while
  249.9 2.9 gather_fusion
  254.8 2.6 fusion.40
  257.5 2.7 fusion.41
  261.7 1.1 constant_dynamic-slice_fusion.20
  263.9 0.9 constant_dynamic-update-slice_fusion.8
  265.4 1.1 constant_dynamic-slice_fusion.23
  269.3 1.1 constant_dynamic-slice_fusion.24
  271.6 0.9 constant_dynamic-update-slice_fusion.10
  273.1 1.1 constant_dynamic-slice_fusion.25
  277.1 5.4 %copy.83 = f32[1024,1024]{1,0:T(8,128)} copy(f32[1024,1024]{0,1:T(8,128)} %get-tuple-element.53) | data formatting | bytes 8388608 | tf_op jit(solution)/shard_map/while | solution.py:116
  282.4 4.7 %copy.84 = f32[2,16,1,32,1024]{4,3,1,0,2:T(8,128)} copy(f32[2,16,1,32,1024]{4,3,0,1,2:T(8,128)} %bitcast.175) | data formatting | bytes 8388608 | tf_op jit(solution)/shard_map/transpose | solution.py:18
  287.2 21.7 %reduce-scatter.3.cloned.1.call-done = f32[16,1,32,1024]{3,2,0,1:T(8,128)} async-done(((f32[32,1,32,1024]{3,2,0,1:T(8,128)}), f32[16,1,32,1024]{3,2,0,1:T(8,128)}) %reduce-scatter.3.cloned.1.call-update) | async-done | bytes 2097168 | tf_op jit(solution)/shard_map/reduce_scatter | solution.py:21
  308.9 78.3 %reduce-scatter.5.cloned.1.call-done = f32[1,1,32,1024]{3,2,0,1:T(8,128)} async-done(((f32[16,1,32,1024]{3,2,0,1:T(8,128)}), f32[1,1,32,1024]{3,2,0,1:T(8,128)}) %reduce-scatter.5.cloned.1.call-update) | async-done | bytes 131088 | tf_op jit(solution)/shard_map/reduce_scatter | solution.py:21
  (99 shorter events, 19.8 us)
Async XLA Ops:
  6.5 19.4 %copy-start = (s32[1,1024]{1,0:T(1,128)S(1)}, s32[1,1024]{1,0:T(1,128)}, u32[]{:S(2)}) copy-start(s32[1,1024]{1,0:T(1,128)} %param.12) | copy-start | bytes 12292
  9.9 15.8 %copy-start.4 = (s32[2,4]{1,0:T(2,128)S(1)}, s32[2,4]{1,0:T(2,128)}, u32[]{:S(2)}) copy-start(s32[2,4]{1,0:T(2,128)} %param.16) | copy-start | bytes 100
  9.9 199.2 %all-to-all-start = ((f32[32,1,32,1024]{3,2,1,0:T(8,128)}), f32[32,1,32,1024]{3,2,1,0:T(8,128)}, u32[]{:S(2)}, u32[]{:S(2)}) async-start(f32[32,1,32,1024]{3,2,1,0:T(8,128)} %stack.2), calls=%async_computation | async-start | bytes 8388608 | tf_op jit(solution)/shard_map/all_to_all | solution.py:91
  25.7 4.8 %copy-start.5 = (f32[1,3,256]{2,0,1:T(1,128)S(1)}, f32[1,3,256]{2,0,1:T(1,128)}, u32[]{:S(2)}) copy-start(f32[1,3,256]{2,0,1:T(1,128)} %param.11) | copy-start | bytes 9220
  25.7 8.0 %copy-start.1 = (f32[1,1024]{1,0:T(1,128)S(1)}, f32[1,1024]{1,0:T(1,128)}, u32[]{:S(2)}) copy-start(f32[1,1024]{1,0:T(1,128)} %param.13) | copy-start | bytes 12292
  25.7 283.2 %reduce-scatter.3.cloned.1.call-start = ((), (), s32[]{:S(2)}) async-start(), calls=%async_computation.3 | async-start | bytes 6291456 | tf_op jit(solution)/shard_map/reduce_scatter | solution.py:21
  33.7 178.0 %copy-start.2 = (f32[2,3,512]{2,0,1:T(2,128)S(1)}, f32[2,3,512]{2,0,1:T(2,128)}, u32[]{:S(2)}) copy-start(f32[2,3,512]{2,0,1:T(2,128)} %param.14) | copy-start | bytes 36868
  33.7 178.0 %copy-start.3 = (f32[2,512]{1,0:T(2,128)S(1)}, f32[2,512]{1,0:T(2,128)}, u32[]{:S(2)}) copy-start(f32[2,512]{1,0:T(2,128)} %param.15) | copy-start | bytes 12292
  287.2 100.1 %reduce-scatter.5.cloned.1.call-start = ((), (), s32[]{:S(2)}) async-start(), calls=%async_computation.4 | async-start | bytes 2228224 | tf_op jit(solution)/shard_map/reduce_scatter | solution.py:21
Sparse Core Ops, SparseCore 0:
  287.3 21.5 reduce-scatter.2
  311.7 75.4 reduce-scatter.4
